TPU v7x, 256 devices: a whole 4x4x8 slice. The times are simulated.
256 devices in a mesh: grp: 32 (over y, x, core), ctx: 8 (over z).
Axes of the slice: x: 4, y: 4, z: 8, core: 2. Of those that a mesh axis runs over, the one named last changes fastest.
Arguments:
- hidden: bfloat16 [65536, 3584], P(('grp', 'ctx')), may hold values from -6 to 6
- norm_gain: float32 [3584], replicated, may hold values from 0.1 to 1.9
- qkv_weight: bfloat16 [3584, 2304], P('grp'), may hold values from -4.008919 to 4.008919
- qkv_bias: float32 [2304], replicated, may hold values from -3 to 3
- repo_lengths: int32 [32, 6], P('grp'), may hold values from 1 to 1024, 2048 in all within a row
Outputs:
- context: bfloat16 [65536, 1792], P(('grp', 'ctx'))
All inputs are finite; a program needn't handle non-finite values.
Results may differ from a plain program's by a relative error of at most 0.0059.
The roundings to bfloat16 on the way count: a program that leaves them out, or rounds other values in their place, can miss the bound.
Values may be sent and summed in bfloat16 or wider, within the bound.
No kernel may reach another device: no remote copies, remote signals or barrier semaphores. Data moves between devices by JAX's collectives and lax.ppermute only.
A program may use at most 128 MiB of HBM per device.

v0:
```python
import jax
import jax.numpy as jnp
from jax import lax
from jax.sharding import PartitionSpec as P

HEAD_DIM = 128
HEADS = 14
KV_HEADS = 2
rope_base = 1000000.0
norm_eps = 1e-06


def rope_tables(position):
    inv_freq = rope_base ** (-jnp.arange(0, HEAD_DIM, 2, dtype=jnp.float32) / HEAD_DIM)
    angle = position.astype(jnp.float32)[:, None] * inv_freq[None, :]
    angle = jnp.concatenate([angle, angle], axis=-1)
    return (jnp.cos(angle), jnp.sin(angle))


def rotate(values, cosine, sine_part):
    half = HEAD_DIM // 2
    first = values[..., :half]
    second = values[..., half:]
    turned = jnp.concatenate([-second, first], axis=-1)
    return values * cosine[:, None, :] + turned * sine_part[:, None, :]


def body(hidden, norm_gain, qkv_weight, qkv_bias, repo_lengths):
    tok_rows = hidden.shape[0]
    group_heads = HEADS // KV_HEADS
    hidden_f32 = hidden.astype(jnp.float32)
    normed = (
        hidden_f32
        * lax.rsqrt(jnp.mean(hidden_f32 * hidden_f32, axis=1, keepdims=True) + norm_eps)
        * norm_gain[None, :]
    ).astype(jnp.bfloat16)
    projected_f32 = jnp.dot(
        normed,
        lax.all_gather(qkv_weight, "grp", axis=0, tiled=True),
        preferred_element_type=jnp.float32,
    )
    projected = (projected_f32 + qkv_bias[None, :]).astype(jnp.bfloat16)
    lengths = repo_lengths[0]
    tok_index = lax.axis_index("ctx") * tok_rows + jnp.arange(tok_rows, dtype=jnp.int32)
    repo_ends = jnp.cumsum(lengths)
    repo_start = jnp.sum(
        jnp.where(tok_index[:, None] >= repo_ends[None, :], lengths[None, :], 0), axis=1
    )
    cosine, sine_part = rope_tables(tok_index - repo_start)
    q_cols = HEADS * HEAD_DIM
    k_cols = KV_HEADS * HEAD_DIM
    query_f32 = projected[:, :q_cols].astype(jnp.float32).reshape(tok_rows, HEADS, HEAD_DIM)
    key_f32 = (
        projected[:, q_cols : q_cols + k_cols]
        .astype(jnp.float32)
        .reshape(tok_rows, KV_HEADS, HEAD_DIM)
    )
    queries = (
        rotate(query_f32, cosine, sine_part)
        .astype(jnp.bfloat16)
        .reshape(tok_rows, KV_HEADS, group_heads, HEAD_DIM)
    )
    keys = rotate(key_f32, cosine, sine_part).astype(jnp.bfloat16).reshape(tok_rows, k_cols)
    values = projected[:, q_cols + k_cols :]
    row_max = jnp.full((KV_HEADS, group_heads, tok_rows), -1e30, jnp.float32)
    key_piece = lax.all_gather(keys, "ctx", axis=0, tiled=True)
    value_piece = lax.all_gather(values, "ctx", axis=0, tiled=True)
    key_count = key_piece.shape[0]
    key_heads = key_piece.reshape(key_count, KV_HEADS, HEAD_DIM)
    value_heads = value_piece.reshape(key_count, KV_HEADS, HEAD_DIM)
    scores = jnp.einsum(
        "rgho,kgo->ghrk", queries, key_heads, preferred_element_type=jnp.float32
    ) * HEAD_DIM ** (-0.5)
    key_index = jnp.arange(key_count, dtype=jnp.int32)
    allowed = (key_index[None, :] <= tok_index[:, None]) & (
        key_index[None, :] >= repo_start[:, None]
    )
    scores = jnp.where(allowed, scores, -1e30)
    new_max = jnp.maximum(row_max, jnp.max(scores, axis=-1))
    weights = jnp.where(allowed, jnp.exp(scores - new_max[..., None]), 0.0)
    new_total = jnp.sum(weights, axis=-1)
    rounded_weights = weights.astype(jnp.bfloat16)
    new_weighted = jnp.einsum(
        "ghrk,kgo->ghro", rounded_weights, value_heads, preferred_element_type=jnp.float32
    )
    result = new_weighted / new_total[..., None]
    return (
        jnp.transpose(result, (2, 0, 1, 3)).reshape(tok_rows, HEADS * HEAD_DIM).astype(jnp.bfloat16)
    )


def solution(mesh):
    in_specs = (P(("grp", "ctx"), None), P(), P("grp", None), P(), P("grp", None))
    out_specs = P(("grp", "ctx"), None)
    return jax.shard_map(body, mesh=mesh, in_specs=in_specs, out_specs=out_specs, check_vma=False)
```

profile of v0, /device:TPU:2, one launch (start us, length us, event | category | flops | bytes accessed | tf_op | source)
XLA Modules:
  0.0 203.0 jit_solution(906771220540744256)
XLA Ops:
  6.5 0.7 all-gather.4.cloned.1.call-update
  7.3 0.8 reduce-window.8
  8.2 0.7 select_reduce_fusion
  9.0 0.5 fusion.26
  9.7 1.9 fusion.7
  11.6 78.2 %all-gather.4.cloned.1.call-done = bf16[3584,2304]{1,0:T(8,128)(2,1)} async-done(((bf16[112,2304]{1,0:T(8,128)(2,1)}), bf16[3584,2304]{1,0:T(8,128)(2,1)}) %all-gather.4.cloned.1.call-update) | async-done | bytes 16515088 | tf_op jit(solution)/shard_map/all_gather | solution.py:39
  89.8 10.7 %fusion.6 = bf16[256,2304]{1,0:T(8,128)(2,1)S(1)} fusion(bf16[3584,2304]{1,0:T(8,128)(2,1)} %all-gather.4.cloned.1.call-done, bf16[256,3584]{1,0:T(8,128)(2,1)} %param.5, f32[3584]{0:T(1024)} %param.6, f32[256]{0:T(256)S(1)} %add_rsqrt_fusion, f32[2304]{0:T(1024)} %param.8), kind=kOutput, calls=%fused_computation.10 | convolution fusion | flops 4232708096 | bytes 19554304 | tf_op jit(solution)/shard_map/dot_general | solution.py:37
  100.5 0.7 slice_convert_fusion.1
  101.3 0.3 slice_negate_fusion.1
  101.7 0.4 maximum_multiply_fusion.1
  102.1 0.7 fusion.24
  102.9 0.2 all-gather.8.cloned.1.call-start
  103.1 0.5 fusion.10
  103.6 1.4 slice_convert_fusion
  105.0 1.8 copy.24
  106.8 1.1 slice_negate_fusion
  107.9 33.4 %all-gather.6.cloned.1.call-done = bf16[2048,256]{1,0:T(8,128)(2,1)} async-done(((bf16[256,256]{1,0:T(8,128)(2,1)}), bf16[2048,256]{1,0:T(8,128)(2,1)}) %all-gather.6.cloned.1.call-update) | async-done | bytes 1048592 | tf_op jit(solution)/shard_map/all_gather | solution.py:66
  141.3 2.1 %reshape.134 = bf16[2048,2,128]{2,1,0:T(2,128)(2,1)} reshape(bf16[2048,256]{1,0:T(8,128)(2,1)} %all-gather.6.cloned.1.call-done) | data formatting | bytes 2097152 | tf_op jit(solution)/shard_map/reshape | solution.py:69
  143.4 13.5 %fusion = (f32[2,7,256]{2,1,0:T(8,128)S(1)}, f32[2,2048,256,7]{2,1,3,0:T(8,128)}) fusion(pred[256,2048]{0,1:T(8,128)(4,1)S(1)} %fusion.10, f32[256,2,7,64]{0,3,2,1:T(8,128)} %bitcast.48, f32[256,2,7,64]{0,3,2,1:T(8,128)S(1)} %bitcast.47, f32[256,2,7,128]{0,3,2,1:T(8,128)S(1)} %bitcast.45, f32[256,128]{0,1:T(8,128)S(1)} %get-tuple-element.12, ...), kind=kOutput, calls=%fused_computation.2 | convolution fusion | flops 1903358464 | bytes 34879488 | tf_op jit(solution)/shard_map/rgho,kgo->ghrk/dot_general | solution.py:71
  156.9 13.5 %fusion.1 = f32[2,7,256]{2,1,0:T(8,128)S(1)} fusion(f32[2,2048,256,7]{2,1,3,0:T(8,128)} %get-tuple-element.14, f32[2,7,256]{2,1,0:T(8,128)S(1)} %broadcast_maximum_fusion, pred[256,2048]{0,1:T(8,128)(4,1)S(1)} %fusion.10), kind=kLoop, calls=%fused_computation.3 | loop fusion | flops 36696576 | bytes 29913088 | tf_op jit(solution)/shard_map/reduce_sum | solution.py:81
  170.5 9.9 %all-gather.8.cloned.1.call-done = bf16[2048,256]{1,0:T(8,128)(2,1)} async-done(((bf16[256,256]{1,0:T(8,128)(2,1)}), bf16[2048,256]{1,0:T(8,128)(2,1)}) %all-gather.8.cloned.1.call-update) | async-done | bytes 1048592 | tf_op jit(solution)/shard_map/all_gather | solution.py:67
  180.3 1.5 copy.37
  181.8 13.3 %fusion.14 = bf16[256,2,7,128]{0,3,2,1:T(8,128)(2,1)S(1)} fusion(bf16[2048,2,128,1]{0,2,3,1:T(8,128)(2,1)S(1)} %bitcast.51, f32[2,2048,256,7]{2,1,3,0:T(8,128)} %get-tuple-element.14, f32[2,7,256]{2,1,0:T(8,128)S(1)} %broadcast_maximum_fusion, pred[256,2048]{0,1:T(8,128)(4,1)S(1)} %fusion.10, f32[256,2,7]{0,2,1:T(8,128)S(1)} %bitcast.53), kind=kOutput, calls=%fused_computation.21 | convolution fusion | flops 1916665856 | bytes 31879168 | tf_op jit(solution)/shard_map/ghrk,kgo->ghro/dot_general | solution.py:83
  195.1 1.4 copy.30
  (14 shorter events, 0.6 us)
Async XLA Ops:
  6.5 83.3 %all-gather.4.cloned.1.call-start = ((), (), s32[]{:S(2)}) async-start(), calls=%async_computation | async-start | bytes 17031168 | tf_op jit(solution)/shard_map/all_gather | solution.py:39
  7.3 134.1 %all-gather.6.cloned.1.call-start = ((), (), s32[]{:S(2)}) async-start(), calls=%async_computation.1 | async-start | bytes 1179648 | tf_op jit(solution)/shard_map/all_gather | solution.py:66
  102.9 77.5 %all-gather.8.cloned.1.call-start = ((), (), s32[]{:S(2)}) async-start(), calls=%async_computation.2 | async-start | bytes 1179648 | tf_op jit(solution)/shard_map/all_gather | solution.py:67
Sparse Core Ops, SparseCore 0:
  9.9 79.8 all-gather.3
  103.0 38.2 all-gather.5
  143.1 37.1 all-gather.7
where the time goes:
time: 203 us
  waiting for transfers between devices  122 us (60%)
  matrix products  37.5 us (18%)
  other arithmetic  22.6 us (11%)
  between operations  13.2 us (7%)
  local copies, waits for them, and re-layouts  7.21 us (4%)
    all_gather x1, waiting for transfers between devices, body(): lax.all_gather(qkv_weight, 'grp', axis=0, tiled=True)  78.2 us
    all_gather x1, waiting for transfers between devices, body(): key_piece = lax.all_gather(keys, 'ctx', axis=0, tiled=True)  33.4 us
    reduce_sum x1, other arithmetic, body(): new_total = jnp.sum(weights, axis=-1)  13.5 us
    dot_general x1, matrix products, body(): jnp.einsum('rgho,kgo->ghrk', queries, key_heads, preferred_element_type=j...  13.5 us
    dot_general x1, matrix products, body(): jnp.einsum('ghrk,kgo->ghro', rounded_weights, value_heads, preferred_elem...  13.3 us
    dot_general x1, matrix products, body(): jnp.dot(normed, lax.all_gather(qkv_weight, 'grp', axis=0, tiled=True), pr...  10.7 us
    all_gather x1, waiting for transfers between devices, body(): value_piece = lax.all_gather(values, 'ctx', axis=0, tiled=True)  9.88 us
  transfers between devices with their start and end apart: 3, of which 3 were waited for; matrix products, arithmetic and copies ran while one was open for 19% of the time, Pallas kernels for 0%

commit v1 on v0

--- a/solution.py
+++ b/solution.py
@@ -64,7 +64,16 @@
     values = projected[:, q_cols + k_cols :]
     row_max = jnp.full((KV_HEADS, group_heads, tok_rows), -1e30, jnp.float32)
     key_piece = lax.all_gather(keys, "ctx", axis=0, tiled=True)
-    value_piece = lax.all_gather(values, "ctx", axis=0, tiled=True)
+    ways = lax.axis_size("ctx")
+    up = [(d, (d + 1) % ways) for d in range(ways)]
+    down = [(d, (d - 1) % ways) for d in range(ways)]
+    earlier, later = ([values], [values])
+    for _ in range(ways // 2):
+        earlier.append(lax.ppermute(earlier[-1], "ctx", up))
+    for _ in range((ways - 1) // 2):
+        later.append(lax.ppermute(later[-1], "ctx", down))
+    line = jnp.concatenate([*earlier[::-1], *later[1:]], axis=0)
+    value_piece = jnp.roll(line, (lax.axis_index("ctx") - ways // 2) * values.shape[0], axis=0)
     key_count = key_piece.shape[0]
     key_heads = key_piece.reshape(key_count, KV_HEADS, HEAD_DIM)
     value_heads = value_piece.reshape(key_count, KV_HEADS, HEAD_DIM)

time: 203 us -> 221 us (1.089)
  starting transfers between devices: 0.26 us -> 11.7 us
  local copies, waits for them, and re-layouts: 7.21 us -> 11.9 us
  waiting for transfers between devices: 122 us -> 125 us
    ppermute x0 -> x7, waiting for transfers between devices: none -> 13.8 us  [the longest x4 13.3 us: body(): earlier.append(lax.ppermute(earlier[-1], 'ctx', up))]
    ppermute x0 -> x7, starting transfers between devices: none -> 11.7 us  [the longest x3 10 us: body(): later.append(lax.ppermute(later[-1], 'ctx', down))]
    all_gather x1 -> x0, waiting for transfers between devices: 9.88 us -> none  [body(): value_piece = lax.all_gather(values, 'ctx', axis=0, tiled=True)]
    all_gather x1, waiting for transfers between devices: 33.4 us -> 29.9 us  [body(): key_piece = lax.all_gather(keys, 'ctx', axis=0, tiled=True)]
    dynamic_slice x0 -> x2, local copies, waits for them, and re-layouts: none -> 3.36 us  [body(): jnp.roll(line, (lax.axis_index('ctx') - ways // 2) * values.shape[0], axi...]
    unnamed x0 -> x38, local copies, waits for them, and re-layouts: none -> 2.81 us
    all_gather x1, waiting for transfers between devices: 78.2 us -> 80.5 us  [body(): lax.all_gather(qkv_weight, 'grp', axis=0, tiled=True)]
  transfers between devices with their start and end apart: 3 -> 9, of which waited for: 3 -> 7; matrix products, arithmetic and copies ran while one was open for 19% -> 5% of each run, Pallas kernels for 0% -> 0%
where the time goes in v1:
time: 221 us; the launch traced here: 220 us
  waiting for transfers between devices  125 us (57%)
  matrix products  37.5 us (17%)
  other arithmetic  20.6 us (9%)
  between operations  13.7 us (6%)
  local copies, waits for them, and re-layouts  11.9 us (5%)
  starting transfers between devices  11.7 us (5%)
    all_gather x1, waiting for transfers between devices, body(): lax.all_gather(qkv_weight, 'grp', axis=0, tiled=True)  80.5 us
    all_gather x1, waiting for transfers between devices, body(): key_piece = lax.all_gather(keys, 'ctx', axis=0, tiled=True)  29.9 us
    reduce_sum x1, other arithmetic, body(): new_total = jnp.sum(weights, axis=-1)  13.5 us
    dot_general x1, matrix products, body(): jnp.einsum('rgho,kgo->ghrk', queries, key_heads, preferred_element_type=j...  13.4 us
    dot_general x1, matrix products, body(): jnp.einsum('ghrk,kgo->ghro', rounded_weights, value_heads, preferred_elem...  13.3 us
    ppermute x4, waiting for transfers between devices, body(): earlier.append(lax.ppermute(earlier[-1], 'ctx', up))  13.3 us
    dot_general x1, matrix products, body(): jnp.dot(normed, lax.all_gather(qkv_weight, 'grp', axis=0, tiled=True), pr...  10.7 us
    ppermute x3, starting transfers between devices, body(): later.append(lax.ppermute(later[-1], 'ctx', down))  10 us
  transfers between devices with their start and end apart: 9, of which 7 were waited for; matrix products, arithmetic and copies ran while one was open for 5% of the time, Pallas kernels for 0%

profile of v1, /device:TPU:2, one launch (start us, length us, event | category | flops | bytes accessed | tf_op | source)
XLA Modules:
  0.0 220.3 jit_solution(206336433242824447)
XLA Ops:
  7.3 1.9 fusion.7
  9.3 80.5 %all-gather.3.cloned.1.call-done = bf16[3584,2304]{1,0:T(8,128)(2,1)} async-done(((bf16[112,2304]{1,0:T(8,128)(2,1)}), bf16[3584,2304]{1,0:T(8,128)(2,1)}) %all-gather.3.cloned.1.call-update) | async-done | bytes 16515088 | tf_op jit(solution)/shard_map/all_gather | solution.py:39
  89.8 10.7 %fusion.6 = bf16[256,2304]{1,0:T(8,128)(2,1)S(1)} fusion(bf16[3584,2304]{1,0:T(8,128)(2,1)} %all-gather.3.cloned.1.call-done, bf16[256,3584]{1,0:T(8,128)(2,1)} %param.5, f32[3584]{0:T(1024)S(1)} %copy-done.10, f32[256]{0:T(256)S(1)} %add_rsqrt_fusion, f32[2304]{0:T(1024)S(1)} %copy-done.11), kind=kOutput, calls=%fused_computation.10 | convolution fusion | flops 4232708096 | bytes 19554304 | tf_op jit(solution)/shard_map/dot_general | solution.py:37
  100.6 1.6 collective-permute-start
  102.2 5.7 %collective-permute-done = bf16[256,256]{1,0:T(8,128)(2,1)S(1)} collective-permute-done((bf16[256,256]{1,0:T(8,128)(2,1)S(1)}, bf16[256,256]{1,0:T(8,128)(2,1)S(1)}, u32[]{:S(2)}, u32[]{:S(2)}) %collective-permute-start) | collective-permute-done | bytes 131104 | tf_op jit(solution)/shard_map/ppermute | solution.py:72
  108.2 3.2 %collective-permute-start.4 = (bf16[256,256]{1,0:T(8,128)(2,1)S(1)}, bf16[256,256]{1,0:T(8,128)(2,1)S(1)}, u32[]{:S(2)}, u32[]{:S(2)}) collective-permute-start(bf16[256,256]{1,0:T(8,128)(2,1)S(1)} %slice.28), channel_id=1, source_target_pairs={{0,7},{1,0},{2,1},{3,2},{4,3},{5,4},{6,5},{7,6},{8,15},{9,8},{10,9... | collective-permute-start | bytes 393224 | tf_op jit(solution)/shard_map/ppermute | solution.py:74
  111.4 2.9 %collective-permute-done.1 = bf16[256,256]{1,0:T(8,128)(2,1)S(1)} collective-permute-done((bf16[256,256]{1,0:T(8,128)(2,1)S(1)}, bf16[256,256]{1,0:T(8,128)(2,1)S(1)}, u32[]{:S(2)}, u32[]{:S(2)}) %collective-permute-start.1) | collective-permute-done | bytes 131104 | tf_op jit(solution)/shard_map/ppermute | solution.py:72
  114.3 3.3 %collective-permute-start.5 = (bf16[256,256]{1,0:T(8,128)(2,1)S(1)}, bf16[256,256]{1,0:T(8,128)(2,1)S(1)}, u32[]{:S(2)}, u32[]{:S(2)}) collective-permute-start(bf16[256,256]{1,0:T(8,128)(2,1)S(1)} %collective-permute-done.4), channel_id=1, source_target_pairs={{0,7},{1,0},{2,1},{3,2},{4,3},{5,4},{6,5},{7,6},{8,15},{9,8},{10,9... | collective-permute-start | bytes 393224 | tf_op jit(solution)/shard_map/ppermute | solution.py:74
  117.6 2.8 %collective-permute-done.2 = bf16[256,256]{1,0:T(8,128)(2,1)S(1)} collective-permute-done((bf16[256,256]{1,0:T(8,128)(2,1)S(1)}, bf16[256,256]{1,0:T(8,128)(2,1)S(1)}, u32[]{:S(2)}, u32[]{:S(2)}) %collective-permute-start.2) | collective-permute-done | bytes 131104 | tf_op jit(solution)/shard_map/ppermute | solution.py:72
  121.2 3.5 %collective-permute-start.6 = (bf16[256,256]{1,0:T(8,128)(2,1)S(1)}, bf16[256,256]{1,0:T(8,128)(2,1)S(1)}, u32[]{:S(2)}, u32[]{:S(2)}) collective-permute-start(bf16[256,256]{1,0:T(8,128)(2,1)S(1)} %collective-permute-done.5), channel_id=1, source_target_pairs={{0,7},{1,0},{2,1},{3,2},{4,3},{5,4},{6,5},{7,6},{8,15},{9,8},{10,9... | collective-permute-start | bytes 393224 | tf_op jit(solution)/shard_map/ppermute | solution.py:74
  124.7 1.9 collective-permute-done.3
  127.9 1.3 copy-done.1
  131.4 1.3 slice_convert_fusion
  132.7 1.8 copy.23
  134.5 1.1 slice_negate_fusion
  135.6 0.8 copy-done.2
  136.5 1.1 constant_dynamic-slice_fusion
  137.6 2.3 %copy.27 = bf16[2048,256]{0,1:T(8,128)(2,1)} copy(bf16[2048,256]{1,0:T(8,128)(2,1)} %constant_dynamic-slice_fusion) | data formatting | bytes 2097152 | tf_op jit(solution)/shard_map/jit(_roll_dynamic)/dynamic_slice | solution.py:76
  139.9 29.9 %all-gather.5.cloned.1.call-done = bf16[2048,256]{1,0:T(8,128)(2,1)} async-done(((bf16[256,256]{1,0:T(8,128)(2,1)}), bf16[2048,256]{1,0:T(8,128)(2,1)}) %all-gather.5.cloned.1.call-update) | async-done | bytes 1048592 | tf_op jit(solution)/shard_map/all_gather | solution.py:66
  169.7 2.1 reshape.134
  171.8 13.4 %fusion = (f32[2,7,256]{2,1,0:T(8,128)S(1)}, f32[2,2048,256,7]{2,1,3,0:T(8,128)}) fusion(pred[256,2048]{0,1:T(8,128)(4,1)S(1)} %fusion.10, f32[256,2,7,64]{0,3,2,1:T(8,128)} %bitcast.48, f32[256,2,7,64]{0,3,2,1:T(8,128)S(1)} %bitcast.47, f32[256,2,7,128]{0,3,2,1:T(8,128)S(1)} %bitcast.45, f32[256,128]{0,1:T(8,128)S(1)} %get-tuple-element.12, ...), kind=kOutput, calls=%fused_computation.2 | convolution fusion | flops 1903358464 | bytes 34879488 | tf_op jit(solution)/shard_map/rgho,kgo->ghrk/dot_general | solution.py:80
  185.3 13.5 %fusion.1 = f32[2,7,256]{2,1,0:T(8,128)S(1)} fusion(f32[2,2048,256,7]{2,1,3,0:T(8,128)} %get-tuple-element.14, f32[2,7,256]{2,1,0:T(8,128)S(1)} %broadcast_maximum_fusion, pred[256,2048]{0,1:T(8,128)(4,1)S(1)} %fusion.10), kind=kLoop, calls=%fused_computation.3 | loop fusion | flops 36696576 | bytes 29913088 | tf_op jit(solution)/shard_map/reduce_sum | solution.py:90
  198.8 13.3 %fusion.14 = bf16[256,2,7,128]{0,3,2,1:T(8,128)(2,1)S(1)} fusion(bf16[2048,2,128,1]{0,2,3,1:T(8,128)(2,1)S(1)} %bitcast.51, f32[2,2048,256,7]{2,1,3,0:T(8,128)} %get-tuple-element.14, f32[2,7,256]{2,1,0:T(8,128)S(1)} %broadcast_maximum_fusion, pred[256,2048]{0,1:T(8,128)(4,1)S(1)} %fusion.10, f32[256,2,7]{0,2,1:T(8,128)S(1)} %bitcast.53), kind=kOutput, calls=%fused_computation.21 | convolution fusion | flops 1916665856 | bytes 31879168 | tf_op jit(solution)/shard_map/ghrk,kgo->ghro/dot_general | solution.py:92
  212.1 1.4 copy.29
  (66 shorter events, 5.1 us)
Async XLA Ops:
  6.5 83.3 %copy-start.11 = (f32[2304]{0:T(1024)S(1)}, f32[2304]{0:T(1024)}, u32[]{:S(2)}) copy-start(f32[2304]{0:T(1024)} %param.8) | copy-start | bytes 27652
  6.5 83.3 %copy-start.10 = (f32[3584]{0:T(1024)S(1)}, f32[3584]{0:T(1024)}, u32[]{:S(2)}) copy-start(f32[3584]{0:T(1024)} %param.6) | copy-start | bytes 43012
  6.5 83.2 %all-gather.3.cloned.1.call-start = ((), (), s32[]{:S(2)}) async-start(), calls=%async_computation | async-start | bytes 17031168 | tf_op jit(solution)/shard_map/all_gather | solution.py:39
  7.3 162.4 %all-gather.5.cloned.1.call-start = ((), (), s32[]{:S(2)}) async-start(), calls=%async_computation.1 | async-start | bytes 1179648 | tf_op jit(solution)/shard_map/all_gather | solution.py:66
  9.3 98.6 %copy-start.9 = (s32[1,6]{1,0:T(1,128)S(1)}, s32[1,6]{1,0:T(1,128)}, u32[]{:S(2)}) copy-start(s32[1,6]{1,0:T(1,128)} %param.9) | copy-start | bytes 76
  100.6 7.3 %collective-permute-start = (bf16[256,256]{1,0:T(8,128)(2,1)S(1)}, bf16[256,256]{1,0:T(8,128)(2,1)S(1)}, u32[]{:S(2)}, u32[]{:S(2)}) collective-permute-start(bf16[256,256]{1,0:T(8,128)(2,1)S(1)} %slice.28), channel_id=1, source_target_pairs={{0,1},{1,2},{2,3},{3,4},{4,5},{5,6},{6,7},{7,0},{8,9},{9,10},{10,1... | collective-permute-start | bytes 393224 | tf_op jit(solution)/shard_map/ppermute | solution.py:72
  107.9 6.4 %collective-permute-start.1 = (bf16[256,256]{1,0:T(8,128)(2,1)S(1)}, bf16[256,256]{1,0:T(8,128)(2,1)S(1)}, u32[]{:S(2)}, u32[]{:S(2)}) collective-permute-start(bf16[256,256]{1,0:T(8,128)(2,1)S(1)} %collective-permute-done), channel_id=1, source_target_pairs={{0,1},{1,2},{2,3},{3,4},{4,5},{5,6},{6,7},{7,0},{8,9},{9,10},{10,1... | collective-permute-start | bytes 393224 | tf_op jit(solution)/shard_map/ppermute | solution.py:72
  108.2 6.1 %collective-permute-start.4 = (bf16[256,256]{1,0:T(8,128)(2,1)S(1)}, bf16[256,256]{1,0:T(8,128)(2,1)S(1)}, u32[]{:S(2)}, u32[]{:S(2)}) collective-permute-start(bf16[256,256]{1,0:T(8,128)(2,1)S(1)} %slice.28), channel_id=1, source_target_pairs={{0,7},{1,0},{2,1},{3,2},{4,3},{5,4},{6,5},{7,6},{8,15},{9,8},{10,9... | collective-permute-start | bytes 393224 | tf_op jit(solution)/shard_map/ppermute | solution.py:74
  114.3 6.2 %collective-permute-start.2 = (bf16[256,256]{1,0:T(8,128)(2,1)S(1)}, bf16[256,256]{1,0:T(8,128)(2,1)S(1)}, u32[]{:S(2)}, u32[]{:S(2)}) collective-permute-start(bf16[256,256]{1,0:T(8,128)(2,1)S(1)} %collective-permute-done.1), channel_id=1, source_target_pairs={{0,1},{1,2},{2,3},{3,4},{4,5},{5,6},{6,7},{7,0},{8,9},{9,10},{10,1... | collective-permute-start | bytes 393224 | tf_op jit(solution)/shard_map/ppermute | solution.py:72
  114.3 13.1 %copy-start.3 = (bf16[256,256]{1,0:T(8,128)(2,1)}, bf16[256,256]{1,0:T(8,128)(2,1)S(1)}, u32[]{:S(2)}) copy-start(bf16[256,256]{1,0:T(8,128)(2,1)S(1)} %collective-permute-done.4) | copy-start | bytes 393220
  114.3 6.9 %collective-permute-start.5 = (bf16[256,256]{1,0:T(8,128)(2,1)S(1)}, bf16[256,256]{1,0:T(8,128)(2,1)S(1)}, u32[]{:S(2)}, u32[]{:S(2)}) collective-permute-start(bf16[256,256]{1,0:T(8,128)(2,1)S(1)} %collective-permute-done.4), channel_id=1, source_target_pairs={{0,7},{1,0},{2,1},{3,2},{4,3},{5,4},{6,5},{7,6},{8,15},{9,8},{10,9... | collective-permute-start | bytes 393224 | tf_op jit(solution)/shard_map/ppermute | solution.py:74
  120.4 6.2 %collective-permute-start.3 = (bf16[256,256]{1,0:T(8,128)(2,1)S(1)}, bf16[256,256]{1,0:T(8,128)(2,1)S(1)}, u32[]{:S(2)}, u32[]{:S(2)}) collective-permute-start(bf16[256,256]{1,0:T(8,128)(2,1)S(1)} %collective-permute-done.2), channel_id=1, source_target_pairs={{0,1},{1,2},{2,3},{3,4},{4,5},{5,6},{6,7},{7,0},{8,9},{9,10},{10,1... | collective-permute-start | bytes 393224 | tf_op jit(solution)/shard_map/ppermute | solution.py:72
  121.2 6.2 %copy-start.5 = (bf16[256,256]{1,0:T(8,128)(2,1)}, bf16[256,256]{1,0:T(8,128)(2,1)S(1)}, u32[]{:S(2)}) copy-start(bf16[256,256]{1,0:T(8,128)(2,1)S(1)} %collective-permute-done.5) | copy-start | bytes 393220
  121.2 6.0 %collective-permute-start.6 = (bf16[256,256]{1,0:T(8,128)(2,1)S(1)}, bf16[256,256]{1,0:T(8,128)(2,1)S(1)}, u32[]{:S(2)}, u32[]{:S(2)}) collective-permute-start(bf16[256,256]{1,0:T(8,128)(2,1)S(1)} %collective-permute-done.5), channel_id=1, source_target_pairs={{0,7},{1,0},{2,1},{3,2},{4,3},{5,4},{6,5},{7,6},{8,15},{9,8},{10,9... | collective-permute-start | bytes 393224 | tf_op jit(solution)/shard_map/ppermute | solution.py:74
  127.2 0.7 copy-start.7
  127.9 1.3 copy-start.1
  134.5 1.9 copy-start.2
  134.5 1.9 copy-start.4
  134.5 1.9 copy-start.6
  134.5 1.9 copy-start.8
  185.3 13.5 %copy-start = (bf16[2048,256]{0,1:T(8,128)(2,1)S(1)}, bf16[2048,256]{0,1:T(8,128)(2,1)}, u32[]{:S(2)}) copy-start(bf16[2048,256]{0,1:T(8,128)(2,1)} %copy.27) | copy-start | bytes 3145732
Sparse Core Ops, SparseCore 0:
  9.9 79.8 all-gather.2
  131.0 38.6 all-gather.4
